TPU v7x, 256 devices: a whole 4x4x8 slice. The times are simulated.
256 devices in a mesh: row: 16 (over y_hi, x, core), col: 16 (over y_lo, z).
Axes of the slice: x: 4, y: 4 (y_hi: 2, y_lo: 2; y = y_hi * 2 + y_lo), z: 8, core: 2. Of those that a mesh axis runs over, the one named last changes fastest.
Arguments:
- amplitudes: bfloat16 [1600, 40960], P('row', 'col'), may hold values from -6 to 6
- integrals: bfloat16 [32768, 40960], P('row', 'col'), may hold values from -0.0390625 to 0.0390625
- row_offsets: int32 [17], replicated, may hold values from 0 to 20438, as said below
- panel_owner: int32 [3], replicated, may hold values from 0 to 15
Outputs:
- residual: float32 [3, 100, 32768], P(None, None, ('row', 'col'))
Inputs may be any that keep to these rules, and one draw needn't show every extreme that they name: row_offsets[0] is 0 and they rise; row block q holds row_offsets[q + 1] - row_offsets[q] live rows, from 512 to 2048, in its first slots; block 0 holds exactly 2048.
All inputs are finite; a program needn't handle non-finite values.
Results may differ from a plain program's by a relative error of at most 0.0003.
Values may be sent and summed in bfloat16 or wider, within the bound.
No kernel may reach another device: no remote copies, remote signals or barrier semaphores. Data moves between devices by JAX's collectives and lax.ppermute only.
A program may use at most 64 MiB of HBM per device.

v0:
```python
import jax
import jax.numpy as jnp
from jax import lax
from jax.sharding import PartitionSpec as P

STEPS = 3


def from_root(block, axis, source):
    block = jnp.where(lax.axis_index(axis) == source, block, jnp.zeros_like(block))
    return lax.psum(block, axis)


def full_product(amp_panel, integrals):
    return lax.dot_general(
        amp_panel, integrals, (((1,), (1,)), ((), ())), preferred_element_type=jnp.float32
    )


def per_device(amplitudes, integrals, row_offsets, panel_owner):
    own_row = lax.axis_index("row")
    live_rows = row_offsets[own_row + 1] - row_offsets[own_row]
    slot_count = integrals.shape[0]
    live_mask = (jnp.arange(slot_count, dtype=jnp.int32) < live_rows).astype(jnp.float32)
    collected = []
    for step in range(STEPS):
        amp_panel = from_root(amplitudes, "row", panel_owner[step])
        product = full_product(amp_panel, integrals)
        term = product * live_mask[None, :]
        collected.append(lax.psum_scatter(term, "col", scatter_dimension=1, tiled=True))
    return jnp.stack(collected)


def solution(mesh):
    return jax.shard_map(
        per_device,
        mesh=mesh,
        in_specs=(P("row", "col"), P("row", "col"), P(), P()),
        out_specs=P(None, None, ("row", "col")),
        check_vma=False,
    )
```

profile of v0, /device:TPU:2, one launch (start us, length us, event | category | flops | bytes accessed | tf_op | source)
XLA Modules:
  0.0 390.7 jit_solution(16907724380133175974)
XLA Ops:
  6.5 0.0 all-reduce.3.cloned.1.call-start
  6.5 1.4 fusion.2
  9.9 2.3 broadcast_select_fusion.2
  12.1 0.0 all-reduce.3.cloned.1.call-update
  12.1 0.0 reduce-scatter.4.cloned.1.call-start
  12.2 1.3 fusion.1
  14.7 143.7 %all-reduce.3.cloned.1.call-done = (bf16[100,2560]{1,0:T(8,128)(2,1)}, bf16[100,2560]{1,0:T(8,128)(2,1)}, bf16[100,2560]{1,0:T(8,128)(2,1)}) async-done(((bf16[100,2560]{1,0:T(8,128)(2,1)}, bf16[100,2560]{1,0:T(8,128)(2,1)}, bf16[100,2560]{1,0:T(8,128)(2,1)}), (bf16[100,2560]{1,0:T(8,128)(2,1)}, bf16[100,2560]{1,0:T(8,128)(2,1)}, bf16[100,2560]{1,0:T(8,128)(2,1)})) %all-reduce.3.cloned.1.call-update) | async-done | bytes 1536016 | tf_op jit(solution)/shard_map/psum | solution.py:11
  158.5 0.0 copy-start.1
  158.5 0.0 copy-start
  158.5 8.5 %convolution_multiply_fusion.2 = f32[100,2048]{1,0:T(8,128)} fusion(bf16[100,2560]{1,0:T(8,128)(2,1)} %get-tuple-element.7, bf16[2048,2560]{1,0:T(8,128)(2,1)} %param.5, f32[2048]{0:T(1024)S(1)} %fusion), kind=kOutput, calls=%fused_computation.2 | convolution fusion | flops 1048780800 | bytes 11825152 | tf_op jit(solution)/shard_map/dot_general | solution.py:15
  166.9 0.0 reduce-scatter.4.cloned.1.call-update
  167.0 0.0 reduce-scatter.6.cloned.1.call-start
  167.0 0.0 copy-done.1
  167.0 8.2 %convolution_multiply_fusion.1 = f32[100,2048]{1,0:T(8,128)} fusion(bf16[100,2560]{1,0:T(8,128)(2,1)S(1)} %copy-done.1, bf16[2048,2560]{1,0:T(8,128)(2,1)} %param.5, f32[2048]{0:T(1024)S(1)} %fusion), kind=kOutput, calls=%fused_computation.1 | convolution fusion | flops 1048780800 | bytes 11825152 | tf_op jit(solution)/shard_map/dot_general | solution.py:15
  175.2 0.0 reduce-scatter.6.cloned.1.call-update
  175.2 0.0 reduce-scatter.8.cloned.1.call-start
  175.3 0.0 copy-done
  175.3 8.2 %convolution_multiply_fusion = f32[100,2048]{1,0:T(8,128)} fusion(bf16[100,2560]{1,0:T(8,128)(2,1)S(1)} %copy-done, bf16[2048,2560]{1,0:T(8,128)(2,1)} %param.5, f32[2048]{0:T(1024)S(1)} %fusion), kind=kOutput, calls=%fused_computation | convolution fusion | flops 1048780800 | bytes 11825152 | tf_op jit(solution)/shard_map/dot_general | solution.py:15
  183.5 0.0 reduce-scatter.8.cloned.1.call-update
  183.5 59.3 %reduce-scatter.4.cloned.1.call-done = f32[100,128]{1,0:T(8,128)} async-done(((f32[100,2048]{1,0:T(8,128)}), f32[100,128]{1,0:T(8,128)}) %reduce-scatter.4.cloned.1.call-update) | async-done | bytes 51216 | tf_op jit(solution)/shard_map/reduce_scatter | solution.py:30
  242.8 69.9 %reduce-scatter.6.cloned.1.call-done = f32[100,128]{1,0:T(8,128)} async-done(((f32[100,2048]{1,0:T(8,128)}), f32[100,128]{1,0:T(8,128)}) %reduce-scatter.6.cloned.1.call-update) | async-done | bytes 51216 | tf_op jit(solution)/shard_map/reduce_scatter | solution.py:30
  312.7 69.9 %reduce-scatter.8.cloned.1.call-done = f32[100,128]{1,0:T(8,128)} async-done(((f32[100,2048]{1,0:T(8,128)}), f32[100,128]{1,0:T(8,128)}) %reduce-scatter.8.cloned.1.call-update) | async-done | bytes 51216 | tf_op jit(solution)/shard_map/reduce_scatter | solution.py:30
  382.6 1.5 pad_maximum_fusion
  (1 shorter events, 0.0 us)
Async XLA Ops:
  6.5 151.9 %all-reduce.3.cloned.1.call-start = ((), (), s32[]{:S(2)}) async-start(), calls=%async_computation.6 | async-start | bytes 3194880 | tf_op jit(solution)/shard_map/psum | solution.py:11
  12.1 230.6 %reduce-scatter.4.cloned.1.call-start = ((), (), s32[]{:S(2)}) async-start(), calls=%async_computation.3 | async-start | bytes 905216 | tf_op jit(solution)/shard_map/reduce_scatter | solution.py:30
  158.5 8.5 %copy-start.1 = (bf16[100,2560]{1,0:T(8,128)(2,1)S(1)}, bf16[100,2560]{1,0:T(8,128)(2,1)}, u32[]{:S(2)}) copy-start(bf16[100,2560]{1,0:T(8,128)(2,1)} %get-tuple-element.6) | copy-start | bytes 1536004
  158.5 16.8 %copy-start = (bf16[100,2560]{1,0:T(8,128)(2,1)S(1)}, bf16[100,2560]{1,0:T(8,128)(2,1)}, u32[]{:S(2)}) copy-start(bf16[100,2560]{1,0:T(8,128)(2,1)} %get-tuple-element.5) | copy-start | bytes 1536004
  167.0 145.7 %reduce-scatter.6.cloned.1.call-start = ((), (), s32[]{:S(2)}) async-start(), calls=%async_computation.4 | async-start | bytes 905216 | tf_op jit(solution)/shard_map/reduce_scatter | solution.py:30
  175.2 207.4 %reduce-scatter.8.cloned.1.call-start = ((), (), s32[]{:S(2)}) async-start(), calls=%async_computation.5 | async-start | bytes 905216 | tf_op jit(solution)/shard_map/reduce_scatter | solution.py:30
Sparse Core Ops, SparseCore 0:
  12.3 146.1 all-reduce.2
  167.1 75.6 reduce-scatter.3
  245.3 67.3 reduce-scatter.5
  315.2 67.3 reduce-scatter.7
where the time goes:
time: 391 us
  waiting for transfers between devices  343 us (88%)
  matrix products  24.8 us (6%)
  between operations  16.3 us (4%)
    reduce_scatter x3, waiting for transfers between devices, per_device(): lax.psum_scatter(term, 'col', scatter_dimension=1, tiled=True)  199 us
    psum x1, waiting for transfers between devices, from_root(): return lax.psum(block, axis)  144 us
    dot_general x3, matrix products, full_product(): lax.dot_general(amp_panel, integrals, (((1,), (1,)), ((), ())), preferred...  24.8 us
  transfers between devices with their start and end apart: 4, of which 4 were waited for; matrix products, arithmetic and copies ran while one was open for 5% of the time, Pallas kernels for 0%

commit v1 on v0

--- a/solution.py
+++ b/solution.py
@@ -8,7 +8,7 @@
 
 def from_root(block, axis, source):
     block = jnp.where(lax.axis_index(axis) == source, block, jnp.zeros_like(block))
-    return lax.psum(block, axis)
+    return jnp.sum(lax.all_gather(block, axis_name=axis), 0)
 
 
 def full_product(amp_panel, integrals):

time: 391 us -> 472 us (1.21)
  waiting for transfers between devices: 343 us -> 408 us
  other arithmetic: 3.8 us -> 18.6 us
    all_gather x0 -> x3, waiting for transfers between devices: none -> 208 us  [from_root(): return jnp.sum(lax.all_gather(block, axis_name=axis), 0)]
    psum x1 -> x0, waiting for transfers between devices: 144 us -> none  [from_root(): return lax.psum(block, axis)]
    reduce_sum x0 -> x3, other arithmetic: none -> 14.8 us  [from_root(): return jnp.sum(lax.all_gather(block, axis_name=axis), 0)]
  transfers between devices with their start and end apart: 4 -> 6, of which waited for: 4 -> 6; matrix products, arithmetic and copies ran while one was open for 5% -> 9% of each run, Pallas kernels for 0% -> 0%
where the time goes in v1:
time: 472 us; the launch traced here: 471 us
  waiting for transfers between devices  408 us (86%)
  matrix products  24.5 us (5%)
  other arithmetic  18.6 us (4%)
  between operations  16.7 us (4%)
    all_gather x3, waiting for transfers between devices, from_root(): return jnp.sum(lax.all_gather(block, axis_name=axis), 0)  208 us
    reduce_scatter x3, waiting for transfers between devices, per_device(): lax.psum_scatter(term, 'col', scatter_dimension=1, tiled=True)  199 us
    dot_general x3, matrix products, full_product(): lax.dot_general(amp_panel, integrals, (((1,), (1,)), ((), ())), preferred...  24.5 us
    reduce_sum x3, other arithmetic, from_root(): return jnp.sum(lax.all_gather(block, axis_name=axis), 0)  14.8 us
  transfers between devices with their start and end apart: 6, of which 6 were waited for; matrix products, arithmetic and copies ran while one was open for 9% of the time, Pallas kernels for 0%

profile of v1, /device:TPU:2, one launch (start us, length us, event | category | flops | bytes accessed | tf_op | source)
XLA Modules:
  0.0 471.1 jit_solution(7438642600142711256)
XLA Ops:
  6.5 0.0 all-gather.14.cloned.1.call-start
  6.5 1.4 fusion.1
  9.8 2.3 select_bitcast_fusion.2
  12.1 0.0 all-gather.14.cloned.1.call-update
  12.1 0.0 all-gather.12.cloned.1.call-start
  12.2 0.7 all-gather.12.cloned.1.call-update
  12.9 0.0 all-gather.10.cloned.1.call-start
  12.9 0.7 all-gather.10.cloned.1.call-update
  13.6 0.0 reduce-scatter.8.cloned.1.call-start
  13.7 1.4 fusion.2
  16.3 76.1 %all-gather.14.cloned.1.call-done = bf16[16,100,2560]{2,1,0:T(8,128)(2,1)} async-done(((bf16[1,100,2560]{2,1,0:T(8,128)(2,1)}), bf16[16,100,2560]{2,1,0:T(8,128)(2,1)}) %all-gather.14.cloned.1.call-update) | async-done | bytes 8192016 | tf_op jit(solution)/shard_map/all_gather | solution.py:11
  92.4 4.9 %reduce_sum.38 = bf16[100,2560]{1,0:T(8,128)(2,1)S(1)} reduce(bf16[16,100,2560]{2,1,0:T(8,128)(2,1)} %all-gather.14.cloned.1.call-done, bf16[]{:T(256)} %constant.14.clone.1), dimensions={0}, to_apply=%region_4.5 | reduce | flops 3840000 | bytes 8704002 | tf_op jit(solution)/shard_map/reduce_sum | solution.py:11
  97.3 8.2 %convolution_multiply_fusion = f32[100,2048]{1,0:T(8,128)} fusion(bf16[100,2560]{1,0:T(8,128)(2,1)S(1)} %reduce_sum.38, bf16[2048,2560]{1,0:T(8,128)(2,1)} %param.5, f32[2048]{0:T(1024)S(1)} %fusion), kind=kOutput, calls=%fused_computation | convolution fusion | flops 1048780800 | bytes 11825152 | tf_op jit(solution)/shard_map/dot_general | solution.py:15
  105.5 0.0 reduce-scatter.8.cloned.1.call-update
  105.5 0.0 reduce-scatter.6.cloned.1.call-start
  105.5 65.9 %all-gather.12.cloned.1.call-done = bf16[16,100,2560]{2,1,0:T(8,128)(2,1)} async-done(((bf16[1,100,2560]{2,1,0:T(8,128)(2,1)}), bf16[16,100,2560]{2,1,0:T(8,128)(2,1)}) %all-gather.12.cloned.1.call-update) | async-done | bytes 8192016 | tf_op jit(solution)/shard_map/all_gather | solution.py:11
  171.4 4.9 %reduce_sum.37 = bf16[100,2560]{1,0:T(8,128)(2,1)S(1)} reduce(bf16[16,100,2560]{2,1,0:T(8,128)(2,1)} %all-gather.12.cloned.1.call-done, bf16[]{:T(256)} %constant.14.clone.1), dimensions={0}, to_apply=%region_2.3 | reduce | flops 3840000 | bytes 8704002 | tf_op jit(solution)/shard_map/reduce_sum | solution.py:11
  176.3 8.2 %convolution_multiply_fusion.1 = f32[100,2048]{1,0:T(8,128)} fusion(bf16[100,2560]{1,0:T(8,128)(2,1)S(1)} %reduce_sum.37, bf16[2048,2560]{1,0:T(8,128)(2,1)} %param.5, f32[2048]{0:T(1024)S(1)} %fusion), kind=kOutput, calls=%fused_computation.1 | convolution fusion | flops 1048780800 | bytes 11825152 | tf_op jit(solution)/shard_map/dot_general | solution.py:15
  184.6 0.0 reduce-scatter.6.cloned.1.call-update
  184.6 0.0 reduce-scatter.4.cloned.1.call-start
  184.7 65.8 %all-gather.10.cloned.1.call-done = bf16[16,100,2560]{2,1,0:T(8,128)(2,1)} async-done(((bf16[1,100,2560]{2,1,0:T(8,128)(2,1)}), bf16[16,100,2560]{2,1,0:T(8,128)(2,1)}) %all-gather.10.cloned.1.call-update) | async-done | bytes 8192016 | tf_op jit(solution)/shard_map/all_gather | solution.py:11
  250.4 4.9 %reduce_sum.36 = bf16[100,2560]{1,0:T(8,128)(2,1)S(1)} reduce(bf16[16,100,2560]{2,1,0:T(8,128)(2,1)} %all-gather.10.cloned.1.call-done, bf16[]{:T(256)} %constant.14.clone.1), dimensions={0}, to_apply=%region_0.1 | reduce | flops 3840000 | bytes 8704002 | tf_op jit(solution)/shard_map/reduce_sum | solution.py:11
  255.4 8.2 %convolution_multiply_fusion.2 = f32[100,2048]{1,0:T(8,128)} fusion(bf16[100,2560]{1,0:T(8,128)(2,1)S(1)} %reduce_sum.36, bf16[2048,2560]{1,0:T(8,128)(2,1)} %param.5, f32[2048]{0:T(1024)S(1)} %fusion), kind=kOutput, calls=%fused_computation.2 | convolution fusion | flops 1048780800 | bytes 11825152 | tf_op jit(solution)/shard_map/dot_general | solution.py:15
  263.5 0.0 reduce-scatter.4.cloned.1.call-update
  263.5 59.7 %reduce-scatter.8.cloned.1.call-done = f32[100,128]{1,0:T(8,128)} async-done(((f32[100,2048]{1,0:T(8,128)}), f32[100,128]{1,0:T(8,128)}) %reduce-scatter.8.cloned.1.call-update) | async-done | bytes 51216 | tf_op jit(solution)/shard_map/reduce_scatter | solution.py:30
  323.2 69.8 %reduce-scatter.6.cloned.1.call-done = f32[100,128]{1,0:T(8,128)} async-done(((f32[100,2048]{1,0:T(8,128)}), f32[100,128]{1,0:T(8,128)}) %reduce-scatter.6.cloned.1.call-update) | async-done | bytes 51216 | tf_op jit(solution)/shard_map/reduce_scatter | solution.py:30
  393.0 69.7 %reduce-scatter.4.cloned.1.call-done = f32[100,128]{1,0:T(8,128)} async-done(((f32[100,2048]{1,0:T(8,128)}), f32[100,128]{1,0:T(8,128)}) %reduce-scatter.4.cloned.1.call-update) | async-done | bytes 51216 | tf_op jit(solution)/shard_map/reduce_scatter | solution.py:30
  462.7 1.5 pad_maximum_fusion
  (1 shorter events, 0.0 us)
Async XLA Ops:
  6.5 85.8 %all-gather.14.cloned.1.call-start = ((), (), s32[]{:S(2)}) async-start(), calls=%async_computation.8 | async-start | bytes 9052160 | tf_op jit(solution)/shard_map/all_gather | solution.py:11
  12.1 159.3 %all-gather.12.cloned.1.call-start = ((), (), s32[]{:S(2)}) async-start(), calls=%async_computation.7 | async-start | bytes 9052160 | tf_op jit(solution)/shard_map/all_gather | solution.py:11
  12.9 237.6 %all-gather.10.cloned.1.call-start = ((), (), s32[]{:S(2)}) async-start(), calls=%async_computation.6 | async-start | bytes 9052160 | tf_op jit(solution)/shard_map/all_gather | solution.py:11
  13.6 309.6 %reduce-scatter.8.cloned.1.call-start = ((), (), s32[]{:S(2)}) async-start(), calls=%async_computation.5 | async-start | bytes 905216 | tf_op jit(solution)/shard_map/reduce_scatter | solution.py:30
  105.5 287.5 %reduce-scatter.6.cloned.1.call-start = ((), (), s32[]{:S(2)}) async-start(), calls=%async_computation.4 | async-start | bytes 905216 | tf_op jit(solution)/shard_map/reduce_scatter | solution.py:30
  184.6 278.1 %reduce-scatter.4.cloned.1.call-start = ((), (), s32[]{:S(2)}) async-start(), calls=%async_computation.3 | async-start | bytes 905216 | tf_op jit(solution)/shard_map/reduce_scatter | solution.py:30
Sparse Core Ops, SparseCore 0:
  12.3 80.0 all-gather.13
  95.1 76.2 all-gather.11
  174.1 76.2 all-gather.9
  252.8 70.3 reduce-scatter.7
  325.8 67.2 reduce-scatter.5
  395.4 67.3 reduce-scatter.3
